TPU v7x, 512 devices: a whole 4x8x8 slice. The times are simulated.
512 devices in a mesh: leaf: 128 (over y, z, core), sub: 4 (over x).
Axes of the slice: x: 4, y: 8, z: 8, core: 2. Of those that a mesh axis runs over, the one named last changes fastest.
Arguments:
- field: float32 [64, 524288], P(None, ('leaf', 'sub')), may hold values from -6 to 6
- coords: float32 [3, 524288], P(None, ('leaf', 'sub')), may hold values from -6 to 6
- basis: float32 [2048, 64, 256], P(('leaf', 'sub')), may hold values from -0.375 to 0.375
- up_transfer: float32 [2048, 64, 64], P(('leaf', 'sub')), may hold values from -0.1875 to 0.1875
- down_transfer: float32 [2048, 64, 64], P(('leaf', 'sub')), may hold values from -0.75 to 0.75
- couplings: float32 [16384, 64, 64], P(('leaf', 'sub')), may hold values from -0.25 to 0.25
- top_coupling: float32 [128, 128, 64, 64], P('leaf', None, 'sub'), may hold values from -0.25 to 0.25
- send_leaf: int32 [128, 4, 128, 1], P('leaf', 'sub'), may hold values from 0 to 3
- list_slot: int32 [2048, 8], P(('leaf', 'sub')), may hold values from 0 to 127, as said below
- list_block: int32 [2048, 8], P(('leaf', 'sub')), may hold values from 0 to 31
Outputs:
- result: float32 [64, 524288], P(None, ('leaf', 'sub'))
Inputs may be any that keep to these rules, and one draw needn't show every extreme that they name: send_leaf[e, s, d, c] is the leaf, among the 4 of device (e, s), whose skeleton fills slot c of what that device sends to device (d, s). `list_slot`: a list entry q names slot q % 1 from the device q // 1 of the leaf axis with the same sub index; where a device's 4 * 8 list entries are at least 128, every slot is named by some entry of that device, else the device's entries are all different. `list_block`: a list entry names one of the 32 coupling blocks of the leaf's own device.
All inputs are finite; a program needn't handle non-finite values.
Results may differ from a plain program's by a relative error of at most 0.0001.
Values sent between devices are 32-bit elements; how exact they have to be, the bound alone decides.
A program may use at most 64 MiB of HBM per device.

v0:
```python
import math
import jax
import jax.numpy as jnp
from jax import lax
from jax.sharding import PartitionSpec as P

highest = lax.Precision.HIGHEST


def extended(block, sides, width):
    for axis, dim in sides:
        count = lax.axis_size(axis)
        forward = [(i, i + 1) for i in range(count - 1)]
        backward = [(target, source) for source, target in forward]
        low = lax.ppermute(
            lax.slice_in_dim(block, block.shape[dim] - width, None, axis=dim), axis, forward
        )
        high = lax.ppermute(lax.slice_in_dim(block, 0, width, axis=dim), axis, backward)
        block = jnp.concatenate([low, block, high], axis=dim)
    return block


def kernel_block(source_points, target_points, leaf_size):
    dist = jnp.zeros((source_points.shape[1], target_points.shape[1]), jnp.float32)
    for component in range(3):
        gap = source_points[component][:, None] - target_points[component][None, :]
        dist = dist + gap * gap
    return jnp.exp(-0.5 * dist) * (1.0 / math.sqrt(leaf_size))


def add_top(rows, coupling_rows):
    return jnp.einsum("epr,erq->pq", rows, coupling_rows, precision=highest)


def far_terms(incoming, list_slot, chosen, rows, rank):
    gathered = incoming.reshape(-1, rows, rank)[list_slot]
    return jnp.einsum("lkpr,lkrq->lpq", gathered, chosen, precision=highest)


def one_product(
    field,
    coords,
    basis,
    up_transfer,
    down_transfer,
    couplings,
    top_coupling,
    send_leaf,
    list_slot,
    list_block,
):
    rhs_count = field.shape[0]
    leaf_count = basis.shape[0]
    rank = basis.shape[1]
    leaf_size = basis.shape[2]
    stacked = jnp.concatenate([field, coords], 0)
    padded = extended(stacked, ((("leaf", "sub"), 1),), leaf_size)
    leaf_field = field.reshape(rhs_count, leaf_count, leaf_size)
    skeleton = jnp.einsum("pla,lra->lpr", leaf_field, basis, precision=highest)
    outgoing = skeleton[send_leaf.reshape(-1)]
    slot_total = outgoing.shape[0]
    chosen = couplings[list_block]
    incoming = lax.all_to_all(
        outgoing.reshape(slot_total, rhs_count * rank),
        "leaf",
        split_axis=0,
        concat_axis=0,
        tiled=True,
    )
    far = far_terms(incoming, list_slot, chosen, rhs_count, rank)

    def near_leaf(position):
        window = lax.dynamic_slice_in_dim(padded, position * leaf_size, 3 * leaf_size, 1)
        own_points = lax.dynamic_slice_in_dim(
            padded[rhs_count:], (position + 1) * leaf_size, leaf_size, 1
        )
        kernels = kernel_block(window[rhs_count:], own_points, leaf_size)
        return jnp.dot(
            window[:rhs_count], kernels, precision=highest, preferred_element_type=jnp.float32
        )

    near = lax.map(near_leaf, jnp.arange(leaf_count, dtype=jnp.int32))
    parent_part = jnp.einsum("lpr,lrq->pq", skeleton, up_transfer, precision=highest)
    quarter = top_coupling.shape[2]
    coupling_rows = top_coupling[0]
    parent = lax.psum(parent_part, "sub")
    row_start = lax.axis_index("sub") * quarter
    rows = lax.dynamic_slice_in_dim(
        lax.all_gather(parent[None], "leaf", axis=0, tiled=True), row_start, quarter, 2
    )
    top_partial = add_top(rows, coupling_rows)
    top_term = lax.psum(top_partial, "sub")
    coef = far + jnp.einsum("pr,lrq->lpq", top_term, down_transfer, precision=highest)
    total = near + jnp.einsum("lpr,lra->lpa", coef, basis, precision=highest)
    return total.transpose(1, 0, 2).reshape(rhs_count, leaf_count * leaf_size)


def local(
    field,
    coords,
    basis,
    up_transfer,
    down_transfer,
    couplings,
    top_coupling,
    send_leaf,
    list_slot,
    list_block,
):
    current = field
    for repeat in range(2):
        current = one_product(
            current,
            coords,
            basis,
            up_transfer,
            down_transfer,
            couplings,
            top_coupling,
            send_leaf,
            list_slot,
            list_block,
        )
    return current


def solution(mesh):
    in_specs = (
        P(None, ("leaf", "sub")),
        P(None, ("leaf", "sub")),
        P(("leaf", "sub"), None, None),
        P(("leaf", "sub"), None, None),
        P(("leaf", "sub"), None, None),
        P(("leaf", "sub"), None, None),
        P("leaf", None, "sub", None),
        P("leaf", "sub", None, None),
        P(("leaf", "sub"), None),
        P(("leaf", "sub"), None),
    )
    out_specs = P(None, ("leaf", "sub"))
    return jax.shard_map(local, mesh=mesh, in_specs=in_specs, out_specs=out_specs, check_vma=False)
```

profile of v0, /device:TPU:16, one launch (start us, length us, event | category | flops | bytes accessed | tf_op | source)
XLA Modules:
  0.0 379.2 jit_solution(1473924243727374704)
XLA Ops:
  6.5 1.5 fusion.52
  8.0 1.2 convolution_bitcast_fusion.9
  9.2 17.7 %psum.28 = f32[1,64,64]{2,1,0:T(8,128)} all-reduce(f32[1,64,64]{2,1,0:T(8,128)S(1)} %convolution_bitcast_fusion.9), channel_id=1, replica_groups=mesh['leaf'=128,'sub'=4] {'sub'}, use_global_device_ids=true, to_apply=%region_2.3 | all-reduce | flops 4096 | bytes 32768 | tf_op jit(solution)/shard_map/psum | solution.py:86
  26.9 0.7 fusion.60
  27.6 0.6 copy-done.12
  28.2 2.8 gather_fusion
  31.0 3.8 copy.27
  34.8 4.1 %copy.28 = f32[128,1,4096]{2,1,0:T(1,128)} copy(f32[128,1,4096]{0,2,1:T(8,128)S(1)} %bitcast.122) | data formatting | bytes 4194304 | tf_op jit(solution)/shard_map/all_to_all | solution.py:63
  38.9 17.8 %all-to-all-start = ((f32[128,1,4096]{2,1,0:T(1,128)}), f32[128,1,4096]{2,1,0:T(1,128)}, u32[]{:S(2)}, u32[]{:S(2)}) async-start(f32[128,1,4096]{2,1,0:T(1,128)} %copy.28), calls=%async_computation | async-start | bytes 4194304 | tf_op jit(solution)/shard_map/all_to_all | solution.py:63
  56.8 1.9 collective-permute-start
  58.8 7.9 %collective-permute-start.1 = (f32[67,256]{1,0:T(8,128)S(1)}, f32[67,256]{1,0:T(8,128)S(1)}, u32[]{:S(2)}, u32[]{:S(2)}) collective-permute-start(f32[67,256]{1,0:T(8,128)S(1)} %get-tuple-element.82), channel_id=1, source_target_pairs={{1,0},{2,1},{3,2},{4,3},{5,4},{6,5},{7,6},{8,7},{9,8},{10,9},{11,1... | collective-permute-start | bytes 205832 | tf_op jit(solution)/shard_map/ppermute | solution.py:18
  66.8 0.6 pad_clamp_fusion
  67.4 0.6 gather_fusion.2
  68.0 36.9 %collective-permute-done = f32[67,256]{1,0:T(8,128)S(1)} collective-permute-done((f32[67,256]{1,0:T(8,128)S(1)}, f32[67,256]{1,0:T(8,128)S(1)}, u32[]{:S(2)}, u32[]{:S(2)}) %collective-permute-start) | collective-permute-done | bytes 68640 | tf_op jit(solution)/shard_map/ppermute | solution.py:15
  105.0 11.9 %while.20 = (s32[]{:T(128)}, f32[4,64,256]{2,1,0:T(8,128)S(1)}, s32[4]{0:T(128)S(1)}, f32[67,1536]{1,0:T(8,128)S(1)}, s32[]{:T(128)}, /*index=5*/s32[1]{0:T(128)...) while((s32[]{:T(128)}, f32[4,64,256]{2,1,0:T(8,128)S(1)}, ...), condition=%wide.region_1.2_spmd, body=%wide.region_0.1_spmd.sunk | while | flops 152961040 | bytes 339289 | solution.py:82
  105.1 0.6 dynamic_slice.31
  107.1 0.9 fusion.91
  108.0 0.6 dynamic_slice.31
  110.1 0.9 fusion.91
  111.0 0.6 dynamic_slice.31
  113.1 0.9 fusion.91
  114.0 0.6 dynamic_slice.31
  116.1 0.9 fusion.91
  117.0 32.6 %all-gather.3.cloned.1.call-done = f32[128,64,64]{2,1,0:T(8,128)} async-done(((f32[1,64,64]{2,1,0:T(8,128)}), f32[128,64,64]{2,1,0:T(8,128)}) %all-gather.3.cloned.1.call-update) | async-done | bytes 2097168 | tf_op jit(solution)/shard_map/all_gather | solution.py:89
  149.6 5.3 %constant_dynamic-slice_fusion.3 = f32[128,64,16]{2,1,0:T(8,128)} fusion(f32[128,64,64]{2,1,0:T(8,128)} %all-gather.3.cloned.1.call-done, s32[]{:T(128)S(6)} %select_n.38), kind=kLoop, calls=%fused_computation.99 | loop fusion | bytes 1048580 | tf_op jit(solution)/shard_map/dynamic_slice | solution.py:88
  154.9 4.0 %copy.41 = f32[128,64,16]{0,1,2:T(8,128)S(1)} copy(f32[128,64,16]{2,1,0:T(8,128)} %constant_dynamic-slice_fusion.3) | data formatting | bytes 1048576
  159.0 0.6 convolution_bitcast_fusion.8
  159.5 17.6 %psum.29 = f32[64,64]{1,0:T(8,128)} all-reduce(f32[64,64]{1,0:T(8,128)S(1)} %convolution_bitcast_fusion.8), channel_id=1, replica_groups=mesh['leaf'=128,'sub'=4] {'sub'}, use_global_device_ids=true, to_apply=%region_3.4 | all-reduce | flops 4096 | bytes 32768 | tf_op jit(solution)/shard_map/psum | solution.py:92
  177.1 5.6 %copy.29 = f32[128,1,4096]{0,2,1:T(8,128)} copy(f32[128,1,4096]{2,1,0:T(1,128)} %all-to-all-done) | data formatting | bytes 4194304 | tf_op jit(solution)/shard_map/all_to_all | solution.py:63
  182.8 5.6 %copy.30 = f32[128,64,64]{2,1,0:T(8,128)} copy(f32[128,64,64]{0,2,1:T(8,128)} %bitcast.123) | data formatting | bytes 4194304 | tf_op jit(solution)/shard_map/reshape | solution.py:36
  188.4 2.9 gather_fusion.1
  191.3 1.1 convolution_bitcast_fusion.5
  192.4 1.0 fusion.49
  193.8 1.3 fusion.55
  195.2 1.2 convolution_bitcast_fusion.7
  196.4 15.0 %psum.30 = f32[1,64,64]{2,1,0:T(8,128)} all-reduce(f32[1,64,64]{2,1,0:T(8,128)S(1)} %convolution_bitcast_fusion.7), channel_id=1, replica_groups=mesh['leaf'=128,'sub'=4] {'sub'}, use_global_device_ids=true, to_apply=%region_6.7 | all-reduce | flops 4096 | bytes 32768 | tf_op jit(solution)/shard_map/psum | solution.py:86
  211.4 2.9 gather_fusion.3
  214.4 4.7 %copy.33 = f32[128,64,64]{0,2,1:T(8,128)} copy(f32[128,64,64]{2,1,0:T(8,128)} %gather_fusion.3) | data formatting | bytes 4194304 | tf_op jit(solution)/shard_map/gather | solution.py:60
  219.1 5.7 %copy.34 = f32[128,1,4096]{2,1,0:T(1,128)} copy(f32[128,1,4096]{0,2,1:T(8,128)} %bitcast.124) | data formatting | bytes 4194304 | tf_op jit(solution)/shard_map/all_to_all | solution.py:63
  224.8 10.4 %all-to-all-start.1 = ((f32[128,1,4096]{2,1,0:T(1,128)}), f32[128,1,4096]{2,1,0:T(1,128)}, u32[]{:S(2)}, u32[]{:S(2)}) async-start(f32[128,1,4096]{2,1,0:T(1,128)} %copy.34), calls=%async_computation.1 | async-start | bytes 4194304 | tf_op jit(solution)/shard_map/all_to_all | solution.py:63
  235.4 2.6 collective-permute-start.2
  238.0 7.2 %collective-permute-start.3 = (f32[67,256]{1,0:T(8,128)S(1)}, f32[67,256]{1,0:T(8,128)S(1)}, u32[]{:S(2)}, u32[]{:S(2)}) collective-permute-start(f32[67,256]{1,0:T(8,128)S(1)} %get-tuple-element.80), channel_id=1, source_target_pairs={{1,0},{2,1},{3,2},{4,3},{5,4},{6,5},{7,6},{8,7},{9,8},{10,9},{11,1... | collective-permute-start | bytes 205832 | tf_op jit(solution)/shard_map/ppermute | solution.py:18
  245.1 40.4 %collective-permute-done.2 = f32[67,256]{1,0:T(8,128)S(1)} collective-permute-done((f32[67,256]{1,0:T(8,128)S(1)}, f32[67,256]{1,0:T(8,128)S(1)}, u32[]{:S(2)}, u32[]{:S(2)}) %collective-permute-start.2) | collective-permute-done | bytes 68640 | tf_op jit(solution)/shard_map/ppermute | solution.py:15
  285.6 11.9 %while.21 = (s32[]{:T(128)}, f32[4,64,256]{2,1,0:T(8,128)S(1)}, s32[4]{0:T(128)S(1)}, f32[67,1536]{1,0:T(8,128)S(1)}, s32[]{:T(128)}, /*index=5*/s32[1]{0:T(128)...) while((s32[]{:T(128)}, f32[4,64,256]{2,1,0:T(8,128)S(1)}, ...), condition=%wide.region_5.6_spmd, body=%wide.region_4.5_spmd.sunk | while | flops 152961040 | bytes 339289 | solution.py:82
  285.6 0.6 dynamic_slice.32
  287.7 0.9 fusion.94
  288.6 0.6 dynamic_slice.32
  290.7 0.9 fusion.94
  291.6 0.6 dynamic_slice.32
  293.6 0.9 fusion.94
  294.6 0.6 dynamic_slice.32
  296.6 0.9 fusion.94
  297.6 29.0 %all-gather.5.cloned.1.call-done = f32[128,64,64]{2,1,0:T(8,128)} async-done(((f32[1,64,64]{2,1,0:T(8,128)}), f32[128,64,64]{2,1,0:T(8,128)}) %all-gather.5.cloned.1.call-update) | async-done | bytes 2097168 | tf_op jit(solution)/shard_map/all_gather | solution.py:89
  326.5 5.3 %constant_dynamic-slice_fusion.2 = f32[128,64,16]{2,1,0:T(8,128)} fusion(f32[128,64,64]{2,1,0:T(8,128)} %all-gather.5.cloned.1.call-done, s32[]{:T(128)S(6)} %select_n.38), kind=kLoop, calls=%fused_computation.98 | loop fusion | bytes 1048580 | tf_op jit(solution)/shard_map/dynamic_slice | solution.py:88
  331.8 4.0 %copy.42 = f32[128,64,16]{0,1,2:T(8,128)S(1)} copy(f32[128,64,16]{2,1,0:T(8,128)} %constant_dynamic-slice_fusion.2) | data formatting | bytes 1048576
  335.9 0.6 convolution_bitcast_fusion.6
  336.4 17.6 %psum.31 = f32[64,64]{1,0:T(8,128)} all-reduce(f32[64,64]{1,0:T(8,128)S(1)} %convolution_bitcast_fusion.6), channel_id=1, replica_groups=mesh['leaf'=128,'sub'=4] {'sub'}, use_global_device_ids=true, to_apply=%region_7.8 | all-reduce | flops 4096 | bytes 32768 | tf_op jit(solution)/shard_map/psum | solution.py:92
  354.0 5.6 %copy.35 = f32[128,1,4096]{0,2,1:T(8,128)} copy(f32[128,1,4096]{2,1,0:T(1,128)} %all-to-all-done.1) | data formatting | bytes 4194304 | tf_op jit(solution)/shard_map/all_to_all | solution.py:63
  359.7 5.6 %copy.36 = f32[128,64,64]{2,1,0:T(8,128)} copy(f32[128,64,64]{0,2,1:T(8,128)} %bitcast.125) | data formatting | bytes 4194304 | tf_op jit(solution)/shard_map/reshape | solution.py:36
  365.3 2.8 gather_fusion.4
  368.1 1.1 convolution_bitcast_fusion.4
  369.2 1.0 fusion.48
  370.6 1.0 add_bitcast_fusion
  371.6 0.7 copy.45
  (82 shorter events, 2.8 us)
Async XLA Ops:
  6.5 60.9 %copy-start = (f32[32,64,64]{2,1,0:T(8,128)S(1)}, f32[32,64,64]{2,1,0:T(8,128)}, u32[]{:S(2)}) copy-start(f32[32,64,64]{2,1,0:T(8,128)} %param.19) | copy-start | bytes 1572868
  6.5 143.1 %all-gather.3.cloned.1.call-start = ((), (), s32[]{:S(2)}) async-start(), calls=%async_computation.2 | async-start | bytes 4227072 | tf_op jit(solution)/shard_map/all_gather | solution.py:89
  27.6 0.6 copy-start.12
  34.8 22.0 %copy-start.7 = (f32[64,1024]{1,0:T(8,128)S(1)}, f32[64,1024]{1,0:T(8,128)}, u32[]{:S(2)}) copy-start(f32[64,1024]{1,0:T(8,128)} %param.14) | copy-start | bytes 786436
  34.8 22.0 %copy-start.10 = (f32[3,1024]{1,0:T(4,128)S(1)}, f32[3,1024]{1,0:T(4,128)}, u32[]{:S(2)}) copy-start(f32[3,1024]{1,0:T(4,128)} %param.15) | copy-start | bytes 36868
  34.8 31.8 %copy-start.13 = (s32[4,8]{1,0:T(4,128)S(1)}, s32[4,8]{1,0:T(4,128)}, u32[]{:S(2)}) copy-start(s32[4,8]{1,0:T(4,128)} %param.22) | copy-start | bytes 388
  34.8 31.9 %copy-start.14 = (s32[4,8]{1,0:T(4,128)S(1)}, s32[4,8]{1,0:T(4,128)}, u32[]{:S(2)}) copy-start(s32[4,8]{1,0:T(4,128)} %param.23) | copy-start | bytes 388
  38.9 138.2 %all-to-all-start = ((f32[128,1,4096]{2,1,0:T(1,128)}), f32[128,1,4096]{2,1,0:T(1,128)}, u32[]{:S(2)}, u32[]{:S(2)}) async-start(f32[128,1,4096]{2,1,0:T(1,128)} %copy.28), calls=%async_computation | async-start | bytes 4194304 | tf_op jit(solution)/shard_map/all_to_all | solution.py:63
  56.7 269.8 %all-gather.5.cloned.1.call-start = ((), (), s32[]{:S(2)}) async-start(), calls=%async_computation.3 | async-start | bytes 4227072 | tf_op jit(solution)/shard_map/all_gather | solution.py:89
  56.8 48.1 %collective-permute-start = (f32[67,256]{1,0:T(8,128)S(1)}, f32[67,256]{1,0:T(8,128)S(1)}, u32[]{:S(2)}, u32[]{:S(2)}) collective-permute-start(f32[67,256]{1,0:T(8,128)S(1)} %get-tuple-element.81), channel_id=1, source_target_pairs={{0,1},{1,2},{2,3},{3,4},{4,5},{5,6},{6,7},{7,8},{8,9},{9,10},{10,1... | collective-permute-start | bytes 205832 | tf_op jit(solution)/shard_map/ppermute | solution.py:15
  58.8 46.2 %collective-permute-start.1 = (f32[67,256]{1,0:T(8,128)S(1)}, f32[67,256]{1,0:T(8,128)S(1)}, u32[]{:S(2)}, u32[]{:S(2)}) collective-permute-start(f32[67,256]{1,0:T(8,128)S(1)} %get-tuple-element.82), channel_id=1, source_target_pairs={{1,0},{2,1},{3,2},{4,3},{5,4},{6,5},{7,6},{8,7},{9,8},{10,9},{11,1... | collective-permute-start | bytes 205832 | tf_op jit(solution)/shard_map/ppermute | solution.py:18
  117.0 37.9 %copy-start.2 = (f32[4,64,256]{2,1,0:T(8,128)}, f32[4,64,256]{2,1,0:T(8,128)S(1)}, u32[]{:S(2)}) copy-start(f32[4,64,256]{2,1,0:T(8,128)S(1)} %get-tuple-element.49) | copy-start | bytes 786436
  154.9 4.0 %copy-start.4 = (f32[1,128,16,64]{1,3,2,0:T(8,128)S(1)}, f32[1,128,16,64]{1,3,2,0:T(8,128)}, u32[]{:S(2)}) copy-start(f32[1,128,16,64]{1,3,2,0:T(8,128)} %param.20) | copy-start | bytes 1572868
  182.8 9.7 %copy-start.8 = (f32[4,64,64]{2,1,0:T(8,128)S(1)}, f32[4,64,64]{2,1,0:T(8,128)}, u32[]{:S(2)}) copy-start(f32[4,64,64]{2,1,0:T(8,128)} %param.18) | copy-start | bytes 196612
  182.8 10.7 %copy-start.1 = (f32[4,64,256]{2,1,0:T(8,128)S(1)}, f32[4,64,256]{2,1,0:T(8,128)}, u32[]{:S(2)}) copy-start(f32[4,64,256]{2,1,0:T(8,128)} %param.16) | copy-start | bytes 786436
  219.1 16.1 %copy-start.3 = (f32[4,64,256]{2,1,0:T(8,128)S(1)}, f32[4,64,256]{2,1,0:T(8,128)}, u32[]{:S(2)}) copy-start(f32[4,64,256]{2,1,0:T(8,128)} %copy-done.2) | copy-start | bytes 786436
  224.8 129.2 %all-to-all-start.1 = ((f32[128,1,4096]{2,1,0:T(1,128)}), f32[128,1,4096]{2,1,0:T(1,128)}, u32[]{:S(2)}, u32[]{:S(2)}) async-start(f32[128,1,4096]{2,1,0:T(1,128)} %copy.34), calls=%async_computation.1 | async-start | bytes 4194304 | tf_op jit(solution)/shard_map/all_to_all | solution.py:63
  235.4 50.2 %collective-permute-start.2 = (f32[67,256]{1,0:T(8,128)S(1)}, f32[67,256]{1,0:T(8,128)S(1)}, u32[]{:S(2)}, u32[]{:S(2)}) collective-permute-start(f32[67,256]{1,0:T(8,128)S(1)} %get-tuple-element.79), channel_id=1, source_target_pairs={{0,1},{1,2},{2,3},{3,4},{4,5},{5,6},{6,7},{7,8},{8,9},{9,10},{10,1... | collective-permute-start | bytes 205832 | tf_op jit(solution)/shard_map/ppermute | solution.py:15
  238.0 47.6 %collective-permute-start.3 = (f32[67,256]{1,0:T(8,128)S(1)}, f32[67,256]{1,0:T(8,128)S(1)}, u32[]{:S(2)}, u32[]{:S(2)}) collective-permute-start(f32[67,256]{1,0:T(8,128)S(1)} %get-tuple-element.80), channel_id=1, source_target_pairs={{1,0},{2,1},{3,2},{4,3},{5,4},{6,5},{7,6},{8,7},{9,8},{10,9},{11,1... | collective-permute-start | bytes 205832 | tf_op jit(solution)/shard_map/ppermute | solution.py:18
  297.5 29.0 %copy-start.6 = (f32[4,64,256]{2,1,0:T(8,128)}, f32[4,64,256]{2,1,0:T(8,128)S(1)}, u32[]{:S(2)}) copy-start(f32[4,64,256]{2,1,0:T(8,128)S(1)} %get-tuple-element.50) | copy-start | bytes 786436
  331.8 4.0 %copy-start.5 = (f32[1,128,16,64]{1,3,2,0:T(8,128)S(1)}, f32[1,128,16,64]{1,3,2,0:T(8,128)}, u32[]{:S(2)}) copy-start(f32[1,128,16,64]{1,3,2,0:T(8,128)} %param.20) | copy-start | bytes 1572868
  359.7 5.6 %copy-start.11 = (s32[1024]{0:T(1024)S(1)}, s32[1024]{0:T(1024)}, u32[]{:S(2)}) copy-start(s32[1024]{0:T(1024)} %get-tuple-element.84) | copy-start | bytes 12292
  359.7 9.5 %copy-start.9 = (f32[4,64,64]{2,1,0:T(8,128)S(1)}, f32[4,64,64]{2,1,0:T(8,128)}, u32[]{:S(2)}) copy-start(f32[4,64,64]{2,1,0:T(8,128)} %param.18) | copy-start | bytes 196612
Sparse Core Ops, SparseCore 0:
  27.1 122.4 all-gather.2
  211.6 114.9 all-gather.4
where the time goes:
time: 381 us; the launch traced here: 379 us
  waiting for transfers between devices  139 us (36%)
  local copies, waits for them, and re-layouts  79.5 us (21%)
  blocking collectives  67.9 us (18%)
  starting transfers between devices  47.8 us (13%)
  matrix products  18.6 us (5%)
  between operations  13.8 us (4%)
  loops' own time  10.3 us (3%)
    ppermute x2, waiting for transfers between devices, extended(): lax.ppermute(lax.slice_in_dim(block, block.shape[dim] - width, None, axis...  77.3 us
    all_gather x2, waiting for transfers between devices, one_product(): lax.all_gather(parent[None], 'leaf', axis=0, tiled=True)  61.6 us
    psum x2, blocking collectives, one_product(): top_term = lax.psum(top_partial, 'sub')  35.2 us
    psum x2, blocking collectives, one_product(): parent = lax.psum(parent_part, 'sub')  32.7 us
    all_to_all x2, starting transfers between devices, one_product(): lax.all_to_all(outgoing.reshape(slot_total, rhs_count * rank), 'leaf', sp...  28.2 us
    all_to_all x4, local copies, waits for them, and re-layouts, one_product(): lax.all_to_all(outgoing.reshape(slot_total, rhs_count * rank), 'leaf', sp...  21 us
    ppermute x2, starting transfers between devices, extended(): lax.ppermute(lax.slice_in_dim(block, 0, width, axis=dim), axis, backward)  15 us
    gather x4, local copies, waits for them, and re-layouts, one_product(): outgoing = skeleton[send_leaf.reshape(-1)]  14.2 us
  transfers between devices with their start and end apart: 8, of which 4 were waited for; matrix products, arithmetic and copies ran while one was open for 16% of the time, Pallas kernels for 0%

commit v1 on v0

--- a/solution.py
+++ b/solution.py
@@ -86,7 +86,12 @@
     parent = lax.psum(parent_part, "sub")
     row_start = lax.axis_index("sub") * quarter
     rows = lax.dynamic_slice_in_dim(
-        lax.all_gather(parent[None], "leaf", axis=0, tiled=True), row_start, quarter, 2
+        jnp.concatenate(
+            lax.all_to_all(jnp.stack(lax.axis_size("leaf") * [parent[None]], 0), "leaf", 0, 0), 0
+        ),
+        row_start,
+        quarter,
+        2,
     )
     top_partial = add_top(rows, coupling_rows)
     top_term = lax.psum(top_partial, "sub")

time: 381 us -> 428 us (1.12)
  the two profiles are of different devices: /device:TPU:16 before, /device:TPU:48 now
where the time goes in v1:
time: 428 us; the launch traced here: 420 us
  waiting for transfers between devices  151 us (35%)
  local copies, waits for them, and re-layouts  90.7 us (21%)
  starting transfers between devices  69.1 us (16%)
  blocking collectives  63 us (15%)
  other arithmetic  19 us (4%)
  matrix products  16 us (4%)
  loops' own time  11.1 us (3%)
    ppermute x2, waiting for transfers between devices, extended(): lax.ppermute(lax.slice_in_dim(block, block.shape[dim] - width, None, axis...  76.2 us
    all_to_all x2, waiting for transfers between devices, one_product(): lax.all_to_all(jnp.stack(lax.axis_size('leaf') * [parent[None]], 0), 'lea...  74.7 us
    psum x2, blocking collectives, one_product(): parent = lax.psum(parent_part, 'sub')  33.4 us
    psum x2, blocking collectives, one_product(): top_term = lax.psum(top_partial, 'sub')  29.6 us
    all_to_all x2, starting transfers between devices, one_product(): lax.all_to_all(jnp.stack(lax.axis_size('leaf') * [parent[None]], 0), 'lea...  28.1 us
    unnamed x40, local copies, waits for them, and re-layouts  26 us
    all_to_all x4, local copies, waits for them, and re-layouts, one_product(): lax.all_to_all(outgoing.reshape(slot_total, rhs_count * rank), 'leaf', sp...  21 us
    all_to_all x2, starting transfers between devices, one_product(): lax.all_to_all(outgoing.reshape(slot_total, rhs_count * rank), 'leaf', sp...  20.7 us
  transfers between devices with their start and end apart: 8, of which 4 were waited for; matrix products, arithmetic and copies ran while one was open for 17% of the time, Pallas kernels for 0%

profile of v1, /device:TPU:48, one launch (start us, length us, event | category | flops | bytes accessed | tf_op | source)
XLA Modules:
  0.0 420.5 jit_solution(2232198041076904299)
XLA Ops:
  0.0 1.5 fusion.54
  1.5 1.2 convolution_bitcast_fusion.9
  2.7 17.1 %psum.28 = f32[64,64]{1,0:T(8,128)S(1)} all-reduce(f32[64,64]{1,0:T(8,128)S(1)} %convolution_bitcast_fusion.9), channel_id=1, replica_groups=mesh['leaf'=128,'sub'=4] {'sub'}, use_global_device_ids=true, to_apply=%region_2.3 | all-reduce | flops 4096 | bytes 32768 | tf_op jit(solution)/shard_map/psum | solution.py:86
  19.9 2.5 broadcast_bitcast_fusion.1
  22.3 5.5 %reshape.149 = f32[128,1,4096]{2,1,0:T(1,128)} reshape(f32[128,1,64,64]{3,2,1,0:T(8,128)} %broadcast_bitcast_fusion.1) | data formatting | bytes 4194304
  27.9 17.8 %all-to-all-start.1 = ((f32[128,1,4096]{2,1,0:T(1,128)}), f32[128,1,4096]{2,1,0:T(1,128)}, u32[]{:S(2)}, u32[]{:S(2)}) async-start(f32[128,1,4096]{2,1,0:T(1,128)} %reshape.149), calls=%async_computation.1 | async-start | bytes 4194304 | tf_op jit(solution)/shard_map/all_to_all | solution.py:90
  46.3 2.7 gather_fusion
  49.1 3.8 copy.27
  52.9 4.0 copy.28
  56.9 38.4 %all-to-all-done.1 = f32[128,1,4096]{2,1,0:T(1,128)} async-done(((f32[128,1,4096]{2,1,0:T(1,128)}), f32[128,1,4096]{2,1,0:T(1,128)}, u32[]{:S(2)}, u32[]{:S(2)}) %all-to-all-start.1) | async-done | bytes 2097184 | tf_op jit(solution)/shard_map/all_to_all | solution.py:90
  95.3 10.4 %all-to-all-start = ((f32[128,1,4096]{2,1,0:T(1,128)}), f32[128,1,4096]{2,1,0:T(1,128)}, u32[]{:S(2)}, u32[]{:S(2)}) async-start(f32[128,1,4096]{2,1,0:T(1,128)} %copy.28), calls=%async_computation | async-start | bytes 4194304 | tf_op jit(solution)/shard_map/all_to_all | solution.py:63
  105.8 1.9 collective-permute-start
  107.7 8.3 %collective-permute-start.1 = (f32[67,256]{1,0:T(8,128)S(1)}, f32[67,256]{1,0:T(8,128)S(1)}, u32[]{:S(2)}, u32[]{:S(2)}) collective-permute-start(f32[67,256]{1,0:T(8,128)S(1)} %get-tuple-element.82), channel_id=1, source_target_pairs={{1,0},{2,1},{3,2},{4,3},{5,4},{6,5},{7,6},{8,7},{9,8},{10,9},{11,1... | collective-permute-start | bytes 205832 | tf_op jit(solution)/shard_map/ppermute | solution.py:18
  116.9 0.6 gather_fusion.2
  117.5 37.1 %collective-permute-done = f32[67,256]{1,0:T(8,128)S(1)} collective-permute-done((f32[67,256]{1,0:T(8,128)S(1)}, f32[67,256]{1,0:T(8,128)S(1)}, u32[]{:S(2)}, u32[]{:S(2)}) %collective-permute-start) | collective-permute-done | bytes 68640 | tf_op jit(solution)/shard_map/ppermute | solution.py:15
  154.7 12.5 %while.20 = (s32[]{:T(128)}, f32[4,64,256]{2,1,0:T(8,128)S(1)}, s32[4]{0:T(128)S(1)}, f32[67,1536]{1,0:T(8,128)S(1)}, s32[]{:T(128)}, /*index=5*/s32[1]{0:T(128)...) while((s32[]{:T(128)}, f32[4,64,256]{2,1,0:T(8,128)S(1)}, ...), condition=%wide.region_1.2_spmd, body=%wide.region_0.1_spmd.sunk | while | flops 152961040 | bytes 339289 | solution.py:82
  154.7 0.6 dynamic_slice.37
  156.9 0.9 fusion.91
  157.8 0.6 dynamic_slice.37
  160.1 0.9 fusion.91
  161.0 0.6 dynamic_slice.37
  163.2 0.9 fusion.91
  164.1 0.6 dynamic_slice.37
  166.3 0.9 fusion.91
  167.8 8.7 %reduce.12 = f32[128,4096]{1,0:T(8,128)} reduce(f32[128,1,4096]{2,1,0:T(1,128)} %all-to-all-done.1, f32[]{:T(128)} %broadcast.98), dimensions={1}, to_apply=%all_to_all.20.reduce_sub_computation | reduce | bytes 4194308 | tf_op jit(solution)/shard_map/all_to_all | solution.py:90
  176.5 4.7 %reshape.150 = f32[128,1,64,64]{3,2,1,0:T(8,128)} reshape(f32[128,4096]{1,0:T(8,128)} %reduce.12) | data formatting | bytes 4194304
  181.2 1.3 constant_dynamic-slice_fusion.3
  183.5 14.6 %psum.29 = f32[64,64]{1,0:T(8,128)S(1)} all-reduce(f32[64,64]{1,0:T(8,128)S(1)} %convolution_bitcast_fusion.8), channel_id=1, replica_groups=mesh['leaf'=128,'sub'=4] {'sub'}, use_global_device_ids=true, to_apply=%region_3.4 | all-reduce | flops 4096 | bytes 32768 | tf_op jit(solution)/shard_map/psum | solution.py:97
  198.1 5.7 %copy.29 = f32[128,1,4096]{0,2,1:T(8,128)} copy(f32[128,1,4096]{2,1,0:T(1,128)} %all-to-all-done) | data formatting | bytes 4194304 | tf_op jit(solution)/shard_map/all_to_all | solution.py:63
  203.8 5.6 %copy.30 = f32[128,64,64]{2,1,0:T(8,128)} copy(f32[128,64,64]{0,2,1:T(8,128)} %bitcast.131) | data formatting | bytes 4194304 | tf_op jit(solution)/shard_map/reshape | solution.py:36
  209.4 2.8 gather_fusion.1
  212.2 1.1 convolution_bitcast_fusion.5
  214.7 16.3 %psum.30 = f32[64,64]{1,0:T(8,128)S(1)} all-reduce(f32[64,64]{1,0:T(8,128)S(1)} %convolution_bitcast_fusion.7), channel_id=1, replica_groups=mesh['leaf'=128,'sub'=4] {'sub'}, use_global_device_ids=true, to_apply=%region_6.7 | all-reduce | flops 4096 | bytes 32768 | tf_op jit(solution)/shard_map/psum | solution.py:86
  231.1 2.5 broadcast_bitcast_fusion
  233.5 5.5 %reshape.151 = f32[128,1,4096]{2,1,0:T(1,128)} reshape(f32[128,1,64,64]{3,2,1,0:T(8,128)} %broadcast_bitcast_fusion) | data formatting | bytes 4194304
  239.1 10.3 %all-to-all-start.3 = ((f32[128,1,4096]{2,1,0:T(1,128)}), f32[128,1,4096]{2,1,0:T(1,128)}, u32[]{:S(2)}, u32[]{:S(2)}) async-start(f32[128,1,4096]{2,1,0:T(1,128)} %reshape.151), calls=%async_computation.3 | async-start | bytes 4194304 | tf_op jit(solution)/shard_map/all_to_all | solution.py:90
  249.4 2.9 gather_fusion.3
  252.3 4.8 %copy.34 = f32[128,64,64]{0,2,1:T(8,128)} copy(f32[128,64,64]{2,1,0:T(8,128)} %gather_fusion.3) | data formatting | bytes 4194304 | tf_op jit(solution)/shard_map/gather | solution.py:60
  257.0 5.7 %copy.35 = f32[128,1,4096]{2,1,0:T(1,128)} copy(f32[128,1,4096]{0,2,1:T(8,128)} %bitcast.132) | data formatting | bytes 4194304 | tf_op jit(solution)/shard_map/all_to_all | solution.py:63
  262.7 36.4 %all-to-all-done.3 = f32[128,1,4096]{2,1,0:T(1,128)} async-done(((f32[128,1,4096]{2,1,0:T(1,128)}), f32[128,1,4096]{2,1,0:T(1,128)}, u32[]{:S(2)}, u32[]{:S(2)}) %all-to-all-start.3) | async-done | bytes 2097184 | tf_op jit(solution)/shard_map/all_to_all | solution.py:90
  299.0 10.4 %all-to-all-start.2 = ((f32[128,1,4096]{2,1,0:T(1,128)}), f32[128,1,4096]{2,1,0:T(1,128)}, u32[]{:S(2)}, u32[]{:S(2)}) async-start(f32[128,1,4096]{2,1,0:T(1,128)} %copy.35), calls=%async_computation.2 | async-start | bytes 4194304 | tf_op jit(solution)/shard_map/all_to_all | solution.py:63
  309.6 1.9 collective-permute-start.2
  311.5 8.1 %collective-permute-start.3 = (f32[67,256]{1,0:T(8,128)S(1)}, f32[67,256]{1,0:T(8,128)S(1)}, u32[]{:S(2)}, u32[]{:S(2)}) collective-permute-start(f32[67,256]{1,0:T(8,128)S(1)} %get-tuple-element.80), channel_id=1, source_target_pairs={{1,0},{2,1},{3,2},{4,3},{5,4},{6,5},{7,6},{8,7},{9,8},{10,9},{11,1... | collective-permute-start | bytes 205832 | tf_op jit(solution)/shard_map/ppermute | solution.py:18
  319.6 39.0 %collective-permute-done.2 = f32[67,256]{1,0:T(8,128)S(1)} collective-permute-done((f32[67,256]{1,0:T(8,128)S(1)}, f32[67,256]{1,0:T(8,128)S(1)}, u32[]{:S(2)}, u32[]{:S(2)}) %collective-permute-start.2) | collective-permute-done | bytes 68640 | tf_op jit(solution)/shard_map/ppermute | solution.py:15
  358.7 12.5 %while.21 = (s32[]{:T(128)}, f32[4,64,256]{2,1,0:T(8,128)S(1)}, s32[4]{0:T(128)S(1)}, f32[67,1536]{1,0:T(8,128)S(1)}, s32[]{:T(128)}, /*index=5*/s32[1]{0:T(128)...) while((s32[]{:T(128)}, f32[4,64,256]{2,1,0:T(8,128)S(1)}, ...), condition=%wide.region_5.6_spmd, body=%wide.region_4.5_spmd.sunk | while | flops 152961040 | bytes 339289 | solution.py:82
  358.7 0.6 dynamic_slice.38
  360.9 0.9 fusion.94
  361.8 0.6 dynamic_slice.38
  364.0 0.9 fusion.94
  365.0 0.6 dynamic_slice.38
  367.2 0.9 fusion.94
  368.1 0.6 dynamic_slice.38
  370.3 0.9 fusion.94
  371.2 8.7 %reduce.13 = f32[128,4096]{1,0:T(8,128)} reduce(f32[128,1,4096]{2,1,0:T(1,128)} %all-to-all-done.3, f32[]{:T(128)} %broadcast.98), dimensions={1}, to_apply=%all_to_all.23.reduce_sub_computation | reduce | bytes 4194308 | tf_op jit(solution)/shard_map/all_to_all | solution.py:90
  379.9 4.7 %reshape.152 = f32[128,1,64,64]{3,2,1,0:T(8,128)} reshape(f32[128,4096]{1,0:T(8,128)} %reduce.13) | data formatting | bytes 4194304
  384.6 1.3 constant_dynamic-slice_fusion.2
  386.9 15.0 %psum.31 = f32[64,64]{1,0:T(8,128)} all-reduce(f32[64,64]{1,0:T(8,128)S(1)} %convolution_bitcast_fusion.6), channel_id=1, replica_groups=mesh['leaf'=128,'sub'=4] {'sub'}, use_global_device_ids=true, to_apply=%region_7.8 | all-reduce | flops 4096 | bytes 32768 | tf_op jit(solution)/shard_map/psum | solution.py:97
  401.9 5.6 %copy.36 = f32[128,1,4096]{0,2,1:T(8,128)} copy(f32[128,1,4096]{2,1,0:T(1,128)} %all-to-all-done.2) | data formatting | bytes 4194304 | tf_op jit(solution)/shard_map/all_to_all | solution.py:63
  407.5 5.7 %copy.37 = f32[128,64,64]{2,1,0:T(8,128)} copy(f32[128,64,64]{0,2,1:T(8,128)} %bitcast.133) | data formatting | bytes 4194304 | tf_op jit(solution)/shard_map/reshape | solution.py:36
  413.2 2.8 gather_fusion.4
  416.0 1.1 convolution_bitcast_fusion.4
  417.1 1.0 fusion.48
  418.5 1.0 add_bitcast_fusion
  419.5 0.7 copy.45
  (93 shorter events, 7.6 us)
Async XLA Ops:
  0.0 116.9 %copy-start = (f32[32,64,64]{2,1,0:T(8,128)S(1)}, f32[32,64,64]{2,1,0:T(8,128)}, u32[]{:S(2)}) copy-start(f32[32,64,64]{2,1,0:T(8,128)} %param.19) | copy-start | bytes 1572868
  22.3 23.3 %copy-start.15 = (s32[1,1,128,1]{2,3,1,0:T(1,128)S(1)}, s32[1,1,128,1]{2,3,1,0:T(1,128)}, u32[]{:S(2)}) copy-start(s32[1,1,128,1]{2,3,1,0:T(1,128)} %param.21) | copy-start | bytes 1540
  27.9 67.5 %all-to-all-start.1 = ((f32[128,1,4096]{2,1,0:T(1,128)}), f32[128,1,4096]{2,1,0:T(1,128)}, u32[]{:S(2)}, u32[]{:S(2)}) async-start(f32[128,1,4096]{2,1,0:T(1,128)} %reshape.149), calls=%async_computation.1 | async-start | bytes 4194304 | tf_op jit(solution)/shard_map/all_to_all | solution.py:90
  45.7 0.6 copy-start.12
  52.9 52.9 %copy-start.6 = (f32[64,1024]{1,0:T(8,128)S(1)}, f32[64,1024]{1,0:T(8,128)}, u32[]{:S(2)}) copy-start(f32[64,1024]{1,0:T(8,128)} %param.14) | copy-start | bytes 786436
  52.9 52.9 %copy-start.9 = (f32[3,1024]{1,0:T(4,128)S(1)}, f32[3,1024]{1,0:T(4,128)}, u32[]{:S(2)}) copy-start(f32[3,1024]{1,0:T(4,128)} %param.15) | copy-start | bytes 36868
  52.9 63.2 %copy-start.13 = (s32[4,8]{1,0:T(4,128)S(1)}, s32[4,8]{1,0:T(4,128)}, u32[]{:S(2)}) copy-start(s32[4,8]{1,0:T(4,128)} %param.23) | copy-start | bytes 388
  52.9 63.3 %copy-start.14 = (s32[4,8]{1,0:T(4,128)S(1)}, s32[4,8]{1,0:T(4,128)}, u32[]{:S(2)}) copy-start(s32[4,8]{1,0:T(4,128)} %param.22) | copy-start | bytes 388
  95.3 102.7 %all-to-all-start = ((f32[128,1,4096]{2,1,0:T(1,128)}), f32[128,1,4096]{2,1,0:T(1,128)}, u32[]{:S(2)}, u32[]{:S(2)}) async-start(f32[128,1,4096]{2,1,0:T(1,128)} %copy.28), calls=%async_computation | async-start | bytes 4194304 | tf_op jit(solution)/shard_map/all_to_all | solution.py:63
  105.8 48.8 %collective-permute-start = (f32[67,256]{1,0:T(8,128)S(1)}, f32[67,256]{1,0:T(8,128)S(1)}, u32[]{:S(2)}, u32[]{:S(2)}) collective-permute-start(f32[67,256]{1,0:T(8,128)S(1)} %get-tuple-element.81), channel_id=1, source_target_pairs={{0,1},{1,2},{2,3},{3,4},{4,5},{5,6},{6,7},{7,8},{8,9},{9,10},{10,1... | collective-permute-start | bytes 205832 | tf_op jit(solution)/shard_map/ppermute | solution.py:15
  107.7 46.9 %collective-permute-start.1 = (f32[67,256]{1,0:T(8,128)S(1)}, f32[67,256]{1,0:T(8,128)S(1)}, u32[]{:S(2)}, u32[]{:S(2)}) collective-permute-start(f32[67,256]{1,0:T(8,128)S(1)} %get-tuple-element.82), channel_id=1, source_target_pairs={{1,0},{2,1},{3,2},{4,3},{5,4},{6,5},{7,6},{8,7},{9,8},{10,9},{11,1... | collective-permute-start | bytes 205832 | tf_op jit(solution)/shard_map/ppermute | solution.py:18
  176.5 6.4 %copy-start.3 = (f32[1,128,16,64]{1,3,2,0:T(8,128)S(1)}, f32[1,128,16,64]{1,3,2,0:T(8,128)}, u32[]{:S(2)}) copy-start(f32[1,128,16,64]{1,3,2,0:T(8,128)} %param.20) | copy-start | bytes 1572868
  203.7 5.6 %copy-start.10 = (s32[1024]{0:T(1024)S(1)}, s32[1024]{0:T(1024)}, u32[]{:S(2)}) copy-start(s32[1024]{0:T(1024)} %get-tuple-element.84) | copy-start | bytes 12292
  203.7 9.6 %copy-start.8 = (f32[4,64,64]{2,1,0:T(8,128)S(1)}, f32[4,64,64]{2,1,0:T(8,128)}, u32[]{:S(2)}) copy-start(f32[4,64,64]{2,1,0:T(8,128)} %param.18) | copy-start | bytes 196612
  203.8 9.9 %copy-start.2 = (f32[4,64,256]{2,1,0:T(8,128)S(1)}, f32[4,64,256]{2,1,0:T(8,128)}, u32[]{:S(2)}) copy-start(f32[4,64,256]{2,1,0:T(8,128)} %param.16) | copy-start | bytes 786436
  209.4 5.0 %copy-start.7 = (f32[4,64,64]{2,1,0:T(8,128)S(1)}, f32[4,64,64]{2,1,0:T(8,128)}, u32[]{:S(2)}) copy-start(f32[4,64,64]{2,1,0:T(8,128)} %param.17) | copy-start | bytes 196612
  239.1 60.0 %all-to-all-start.3 = ((f32[128,1,4096]{2,1,0:T(1,128)}), f32[128,1,4096]{2,1,0:T(1,128)}, u32[]{:S(2)}, u32[]{:S(2)}) async-start(f32[128,1,4096]{2,1,0:T(1,128)} %reshape.151), calls=%async_computation.3 | async-start | bytes 4194304 | tf_op jit(solution)/shard_map/all_to_all | solution.py:90
  299.0 102.9 %all-to-all-start.2 = ((f32[128,1,4096]{2,1,0:T(1,128)}), f32[128,1,4096]{2,1,0:T(1,128)}, u32[]{:S(2)}, u32[]{:S(2)}) async-start(f32[128,1,4096]{2,1,0:T(1,128)} %copy.35), calls=%async_computation.2 | async-start | bytes 4194304 | tf_op jit(solution)/shard_map/all_to_all | solution.py:63
  309.6 49.0 %collective-permute-start.2 = (f32[67,256]{1,0:T(8,128)S(1)}, f32[67,256]{1,0:T(8,128)S(1)}, u32[]{:S(2)}, u32[]{:S(2)}) collective-permute-start(f32[67,256]{1,0:T(8,128)S(1)} %get-tuple-element.79), channel_id=1, source_target_pairs={{0,1},{1,2},{2,3},{3,4},{4,5},{5,6},{6,7},{7,8},{8,9},{9,10},{10,1... | collective-permute-start | bytes 205832 | tf_op jit(solution)/shard_map/ppermute | solution.py:15
  311.5 47.1 %collective-permute-start.3 = (f32[67,256]{1,0:T(8,128)S(1)}, f32[67,256]{1,0:T(8,128)S(1)}, u32[]{:S(2)}, u32[]{:S(2)}) collective-permute-start(f32[67,256]{1,0:T(8,128)S(1)} %get-tuple-element.80), channel_id=1, source_target_pairs={{1,0},{2,1},{3,2},{4,3},{5,4},{6,5},{7,6},{8,7},{9,8},{10,9},{11,1... | collective-permute-start | bytes 205832 | tf_op jit(solution)/shard_map/ppermute | solution.py:18
  371.2 13.3 %copy-start.5 = (f32[4,64,256]{2,1,0:T(8,128)}, f32[4,64,256]{2,1,0:T(8,128)S(1)}, u32[]{:S(2)}) copy-start(f32[4,64,256]{2,1,0:T(8,128)S(1)} %get-tuple-element.50) | copy-start | bytes 786436
  379.9 6.4 %copy-start.4 = (f32[1,128,16,64]{1,3,2,0:T(8,128)S(1)}, f32[1,128,16,64]{1,3,2,0:T(8,128)}, u32[]{:S(2)}) copy-start(f32[1,128,16,64]{1,3,2,0:T(8,128)} %param.20) | copy-start | bytes 1572868
  407.5 5.7 %copy-start.11 = (s32[1024]{0:T(1024)S(1)}, s32[1024]{0:T(1024)}, u32[]{:S(2)}) copy-start(s32[1024]{0:T(1024)} %get-tuple-element.84) | copy-start | bytes 12292
  407.5 12.7 %copy-start.1 = (f32[32,64,64]{2,1,0:T(8,128)S(1)}, f32[32,64,64]{2,1,0:T(8,128)}, u32[]{:S(2)}) copy-start(f32[32,64,64]{2,1,0:T(8,128)} %param.19) | copy-start | bytes 1572868
